TPU v7x, 32 devices: a whole 2x2x4 slice. The times are simulated.
32 devices in a mesh: dp: 4 (over y, core), tensor: 8 (over z, x).
Axes of the slice: x: 2, y: 2, z: 4, core: 2. Of those that a mesh axis runs over, the one named last changes fastest.
Arguments:
- hidden_in: bfloat16 [3072, 2048], P(('dp', 'tensor')), may hold values from -6 to 6
- norm1_gain: bfloat16 [2048], replicated, may hold values from 0.099609375 to 1.8984375
- norm2_gain: bfloat16 [2048], replicated, may hold values from 0.099609375 to 1.8984375
- w_query: bfloat16 [2048, 2048], P(None, 'tensor'), may hold values from -0.125 to 0.125
- w_keyval: bfloat16 [2048, 256], replicated, may hold values from -0.125 to 0.125
- w_out: bfloat16 [2048, 2048], P('tensor'), may hold values from -0.5 to 0.5
- w_fc: bfloat16 [2048, 8192], P(None, 'tensor'), may hold values from -0.125 to 0.125
- w_proj: bfloat16 [8192, 2048], P('tensor'), may hold values from -0.0625 to 0.0625
- prefix_kv: bfloat16 [4, 4096, 256], P('dp', 'tensor'), may hold values from -320 to 320
- owner_ids: int32 [4], replicated, may hold values from 0 to 3, each once
- segment_ids: int32 [4, 768], P('dp'), may hold values from 0 to 11, never falling along the last dimension, each value on 1 to 192 neighbouring positions
Outputs:
- layer_out: bfloat16 [3072, 2048], P(('dp', 'tensor'))
- attended: bfloat16 [3072, 2048], P(('dp', 'tensor'))
Inputs may be any that keep to these rules, and one draw needn't show every extreme that they name: `owner_ids`: each stored prefix is extended by exactly one group. `segment_ids`: within a group the request ids never fall; every one of the 12 requests has 1 to 192 tokens, and at least one has exactly 192.
All inputs are finite; a program needn't handle non-finite values.
Results may differ from a plain program's by a relative error of at most 0.015.
Values may be sent and summed in bfloat16 or wider, within the bound.
A program may use at most 128 MiB of HBM per device.

v0:
```python
import math

import jax
import jax.numpy as jnp
from jax import lax
from jax.sharding import PartitionSpec as P


def layer_norm(values, scales):
    widened = values.astype(jnp.float32)
    centre = jnp.mean(widened, axis=-1, keepdims=True)
    centred = widened - centre
    variance = jnp.mean(centred * centred, axis=-1, keepdims=True)
    return (centred * lax.rsqrt(variance + 1e-05) * scales.astype(jnp.float32)).astype(jnp.bfloat16)


def attend_block(state_in, queries, key_rows, value_rows, allowed):
    running, totals, weighted = state_in
    scores = jnp.einsum("htd,kd->htk", queries, key_rows, preferred_element_type=jnp.float32)
    if allowed is not None:
        scores = jnp.where(allowed[None], scores, -jnp.inf)
    new_top = jnp.maximum(running, jnp.max(scores, axis=-1))
    factor = jnp.exp(running - new_top)
    probs = jnp.exp(scores - new_top[..., None])
    totals = totals * factor + jnp.sum(probs, axis=-1)
    probs_b = probs.astype(jnp.bfloat16)
    weighted = weighted * factor[..., None] + jnp.einsum(
        "htk,kd->htd", probs_b, value_rows, preferred_element_type=jnp.float32
    )
    return (new_top, totals, weighted)


def local(
    hidden_in,
    norm1_gain,
    norm2_gain,
    w_query,
    w_keyval,
    w_out,
    w_fc,
    w_proj,
    prefix_kv,
    owner_ids,
    segment_ids,
):
    head_size = w_keyval.shape[1] // 2
    query_cols = w_query.shape[1]
    heads_here = query_cols // head_size
    row_len = segment_ids.shape[1]
    q_scale = 1.0 / math.sqrt(head_size)
    w_joint = jnp.concatenate([w_query, w_keyval], axis=1)
    col_scale = jnp.concatenate(
        [jnp.full((query_cols,), q_scale, jnp.float32), jnp.ones((2 * head_size,), jnp.float32)]
    )
    normed = layer_norm(hidden_in, norm1_gain)
    projected = (
        jnp.dot(
            lax.all_gather(normed, "tensor", axis=0, tiled=True),
            w_joint,
            preferred_element_type=jnp.float32,
        )
        * col_scale
    ).astype(jnp.bfloat16)
    group_here = owner_ids[lax.axis_index("dp")]
    fragment = lax.all_gather(prefix_kv, "dp", axis=0, tiled=True)
    span_len = fragment.shape[0]
    match_rows = jnp.arange(span_len, dtype=jnp.int32) == group_here
    cached = jnp.sum(
        jnp.where(match_rows[:, None, None], fragment, jnp.zeros_like(fragment)), axis=0
    )
    queries = projected[:, :query_cols].reshape(row_len, heads_here, head_size).transpose(1, 0, 2)
    suffix_keys = projected[:, query_cols : query_cols + head_size]
    suffix_values = projected[:, query_cols + head_size :]
    request_ids = segment_ids[0]
    positions = jnp.arange(row_len, dtype=jnp.int32)
    allowed = (positions[None, :] <= positions[:, None]) & (
        request_ids[None, :] == request_ids[:, None]
    )
    start_state = (
        jnp.full((heads_here, row_len), -jnp.inf, jnp.float32),
        jnp.zeros((heads_here, row_len), jnp.float32),
        jnp.zeros((heads_here, row_len, head_size), jnp.float32),
    )
    suffix_state = attend_block(start_state, queries, suffix_keys, suffix_values, allowed)
    fragment = lax.all_gather(cached, "tensor", axis=0, tiled=True)
    state_out = suffix_state
    for row_begin in range(0, fragment.shape[0], 1024):
        block_rows = fragment[row_begin : row_begin + 1024]
        state_out = attend_block(
            state_out, queries, block_rows[:, :head_size], block_rows[:, head_size:], None
        )
    running, totals, weighted = state_out
    attn_heads = (
        (weighted / totals[..., None])
        .astype(jnp.bfloat16)
        .transpose(1, 0, 2)
        .reshape(row_len, query_cols)
    )
    term = jnp.dot(attn_heads, w_out, preferred_element_type=jnp.float32)
    attended = lax.psum_scatter(
        term.astype(jnp.bfloat16).astype(jnp.float32).astype(jnp.bfloat16),
        "tensor",
        scatter_dimension=0,
        tiled=True,
    )
    middle = (hidden_in.astype(jnp.float32) + attended.astype(jnp.float32)).astype(jnp.bfloat16)
    normed2 = layer_norm(middle, norm2_gain)
    hidden_act = jax.nn.gelu(
        jnp.dot(
            lax.all_gather(normed2, "tensor", axis=0, tiled=True),
            w_fc,
            preferred_element_type=jnp.float32,
        ),
        approximate=True,
    ).astype(jnp.bfloat16)
    term = jnp.dot(hidden_act, w_proj, preferred_element_type=jnp.float32)
    mlp_sum = lax.psum_scatter(
        term.astype(jnp.bfloat16).astype(jnp.float32).astype(jnp.bfloat16),
        "tensor",
        scatter_dimension=0,
        tiled=True,
    ).astype(jnp.float32)
    layer_out = (middle.astype(jnp.float32) + mlp_sum).astype(jnp.bfloat16)
    return (layer_out, attended)


def solution(mesh):
    return jax.shard_map(
        local,
        mesh=mesh,
        in_specs=(
            P(("dp", "tensor"), None),
            P(),
            P(),
            P(None, "tensor"),
            P(),
            P("tensor", None),
            P(None, "tensor"),
            P("tensor", None),
            P("dp", "tensor", None),
            P(),
            P("dp", None),
        ),
        out_specs=(P(("dp", "tensor"), None), P(("dp", "tensor"), None)),
        check_vma=False,
    )
```

profile of v0, /device:TPU:0, one launch (start us, length us, event | category | flops | bytes accessed | tf_op | source)
XLA Modules:
  0.0 392.4 jit_solution(12325680166661259745)
XLA Ops:
  9.8 1.3 fusion.102
  11.1 2.0 fusion.104
  13.2 1.2 dynamic_slice.3
  15.1 13.9 %all-gather.7.cloned.1.call-done = bf16[4,512,256]{2,1,0:T(8,128)(2,1)} async-done(((bf16[1,512,256]{2,1,0:T(8,128)(2,1)}), bf16[4,512,256]{2,1,0:T(8,128)(2,1)}) %all-gather.7.cloned.1.call-update) | async-done | bytes 1048592 | tf_op jit(solution)/shard_map/all_gather | solution.py:65
  29.1 2.2 select_reduce_fusion.1
  32.4 59.8 %all-gather.5.cloned.1.call-done = bf16[768,2048]{1,0:T(8,128)(2,1)} async-done(((bf16[96,2048]{1,0:T(8,128)(2,1)}), bf16[768,2048]{1,0:T(8,128)(2,1)}) %all-gather.5.cloned.1.call-update) | async-done | bytes 3145744 | tf_op jit(solution)/shard_map/all_gather | solution.py:58
  92.3 4.0 %multiply_convert_fusion = bf16[768,512]{0,1:T(8,128)(2,1)S(1)} fusion(bf16[768,2048]{1,0:T(8,128)(2,1)} %all-gather.5.cloned.1.call-done, bf16[2048,256]{1,0:T(8,128)(2,1)S(1)} %copy-done.5, bf16[2048,256]{1,0:T(8,128)(2,1)} %param.14, f32[512]{0:T(512)S(1)} %copy-done.6), kind=kOutput, calls=%fused_computation.49 | convolution fusion | flops 1615593472 | bytes 6031360 | tf_op jit(solution)/shard_map/dot_general | solution.py:57
  97.6 2.1 copy-done.1
  100.6 42.3 %all-gather.9.cloned.1.call-done = bf16[4096,256]{1,0:T(8,128)(2,1)} async-done(((bf16[512,256]{1,0:T(8,128)(2,1)}), bf16[4096,256]{1,0:T(8,128)(2,1)}) %all-gather.9.cloned.1.call-update) | async-done | bytes 2097168 | tf_op jit(solution)/shard_map/all_gather | solution.py:85
  142.9 2.2 fusion.136
  148.3 2.6 fusion
  150.9 2.4 fusion.4
  153.4 1.3 fusion.50
  154.7 1.3 fusion.53
  155.9 1.3 fusion.56
  157.2 1.3 fusion.59
  158.5 1.6 fusion.92
  160.1 2.7 convolution_convert_fusion.1
  162.9 72.9 %reduce-scatter.3.cloned.1.call-done = bf16[96,2048]{1,0:T(8,128)(2,1)} async-done(((bf16[768,2048]{1,0:T(8,128)(2,1)}), bf16[96,2048]{1,0:T(8,128)(2,1)}) %reduce-scatter.3.cloned.1.call-update) | async-done | bytes 393232 | tf_op jit(solution)/shard_map/reduce_scatter | solution.py:100
  235.8 1.2 convert_reduce_fusion
  238.4 59.6 %all-gather.11.cloned.1.call-done = bf16[768,2048]{1,0:T(8,128)(2,1)} async-done(((bf16[96,2048]{1,0:T(8,128)(2,1)}), bf16[768,2048]{1,0:T(8,128)(2,1)}) %all-gather.11.cloned.1.call-update) | async-done | bytes 3145744 | tf_op jit(solution)/shard_map/all_gather | solution.py:110
  298.0 12.5 %convolution_convert_fusion = bf16[768,2048]{1,0:T(8,128)(2,1)} fusion(bf16[1024,2048]{1,0:T(8,128)(2,1)} %param.18, bf16[768,2048]{1,0:T(8,128)(2,1)} %all-gather.11.cloned.1.call-done, bf16[2048,1024]{1,0:T(8,128)(2,1)} %param.17), kind=kOutput, calls=%fused_computation.17 | convolution fusion | flops 6451101696 | bytes 14680064 | tf_op jit(solution)/shard_map/dot_general | solution.py:116
  310.6 73.2 %reduce-scatter.5.cloned.1.call-done = bf16[96,2048]{1,0:T(8,128)(2,1)} async-done(((bf16[768,2048]{1,0:T(8,128)(2,1)}), bf16[96,2048]{1,0:T(8,128)(2,1)}) %reduce-scatter.5.cloned.1.call-update) | async-done | bytes 393232 | tf_op jit(solution)/shard_map/reduce_scatter | solution.py:117
  383.8 1.8 fusion.106
  (51 shorter events, 11.4 us)
Async XLA Ops:
  7.2 152.9 %copy-start = (bf16[256,2048]{1,0:T(8,128)(2,1)S(1)}, bf16[256,2048]{1,0:T(8,128)(2,1)}, u32[]{:S(2)}) copy-start(bf16[256,2048]{1,0:T(8,128)(2,1)} %param.16) | copy-start | bytes 3145732
  7.2 85.1 %copy-start.6 = (f32[512]{0:T(512)S(1)}, f32[512]{0:T(512)}, u32[]{:S(2)}) copy-start(f32[512]{0:T(512)} %constant.8.clone.1) | copy-start | bytes 6148
  7.2 85.1 %copy-start.5 = (bf16[2048,256]{1,0:T(8,128)(2,1)S(1)}, bf16[2048,256]{1,0:T(8,128)(2,1)}, u32[]{:S(2)}) copy-start(bf16[2048,256]{1,0:T(8,128)(2,1)} %param.15) | copy-start | bytes 3145732
  7.2 21.9 %all-gather.7.cloned.1.call-start = ((), (), s32[]{:S(2)}) async-start(), calls=%async_computation.3 | async-start | bytes 1310720 | tf_op jit(solution)/shard_map/all_gather | solution.py:65
  7.9 84.4 %all-gather.5.cloned.1.call-start = ((), (), s32[]{:S(2)}) async-start(), calls=%async_computation.2 | async-start | bytes 3538944 | tf_op jit(solution)/shard_map/all_gather | solution.py:58
  13.2 129.8 %all-gather.9.cloned.1.call-start = ((), (), s32[]{:S(2)}) async-start(), calls=%async_computation.4 | async-start | bytes 2359296 | tf_op jit(solution)/shard_map/all_gather | solution.py:85
  31.3 204.5 %reduce-scatter.3.cloned.1.call-start = ((), (), s32[]{:S(2)}) async-start(), calls=%async_computation.5 | async-start | bytes 3538944 | tf_op jit(solution)/shard_map/reduce_scatter | solution.py:100
  97.6 2.1 copy-start.1
  142.9 2.2 copy-start.3
  154.7 3.8 slice-start
  155.9 2.5 slice-start.1
  160.1 2.8 copy-start.4
  160.1 75.7 %copy-start.2 = (bf16[96,2048]{1,0:T(8,128)(2,1)S(1)}, bf16[96,2048]{1,0:T(8,128)(2,1)}, u32[]{:S(2)}) copy-start(bf16[96,2048]{1,0:T(8,128)(2,1)} %param.11) | copy-start | bytes 1179652
  162.8 135.2 %all-gather.11.cloned.1.call-start = ((), (), s32[]{:S(2)}) async-start(), calls=%async_computation.6 | async-start | bytes 3538944 | tf_op jit(solution)/shard_map/all_gather | solution.py:110
  238.4 145.4 %reduce-scatter.5.cloned.1.call-start = ((), (), s32[]{:S(2)}) async-start(), calls=%async_computation.7 | async-start | bytes 3538944 | tf_op jit(solution)/shard_map/reduce_scatter | solution.py:117
Sparse Core Ops, SparseCore 0:
  9.6 19.4 all-gather.6
  31.8 60.4 all-gather.4
  95.0 47.9 all-gather.8
  162.9 72.8 reduce-scatter.2
  238.5 59.5 all-gather.10
  310.7 73.0 reduce-scatter.4
where the time goes:
time: 393 us; the launch traced here: 392 us
  waiting for transfers between devices  323 us (82%)
  matrix products  32.1 us (8%)
  other arithmetic  19.4 us (5%)
  between operations  14.4 us (4%)
    reduce_scatter x2, waiting for transfers between devices, local(): lax.psum_scatter(term.astype(jnp.bfloat16).astype(jnp.float32).astype(jnp...  146 us
    all_gather x1, waiting for transfers between devices, local(): lax.all_gather(normed, 'tensor', axis=0, tiled=True)  59.8 us
    all_gather x1, waiting for transfers between devices, local(): lax.all_gather(normed2, 'tensor', axis=0, tiled=True)  59.6 us
    all_gather x1, waiting for transfers between devices, local(): fragment = lax.all_gather(cached, 'tensor', axis=0, tiled=True)  42.3 us
    all_gather x1, waiting for transfers between devices, local(): fragment = lax.all_gather(prefix_kv, 'dp', axis=0, tiled=True)  13.9 us
    dot_general x1, matrix products, local(): term = jnp.dot(hidden_act, w_proj, preferred_element_type=jnp.float32)  12.5 us
  transfers between devices with their start and end apart: 6, of which 6 were waited for; matrix products, arithmetic and copies ran while one was open for 4% of the time, Pallas kernels for 0%

commit v1 on v0

v1 whole, which is shorter than its diff:
```python
import functools
import math

import jax
import jax.numpy as jnp
from jax import lax
from jax.experimental import pallas as pl
from jax.experimental.pallas import tpu as pltpu
from jax.sharding import PartitionSpec as P

MESH = pl.DeviceIdType.MESH
ROWS = 16


def plane(n):
    lines = 4 if n % 4 == 0 else n
    return lines, n // lines


def norm_rows(widened, gains):
    centre = jnp.mean(widened, axis=-1, keepdims=True)
    centred = widened - centre
    variance = jnp.mean(centred * centred, axis=-1, keepdims=True)
    return (centred * lax.rsqrt(variance + 1e-05) * gains).astype(jnp.bfloat16)


def row_loop(rows, body):
    def step(i, carry):
        body(pl.ds(pl.multiple_of(i * ROWS, ROWS), ROWS))
        return carry

    lax.fori_loop(0, rows // ROWS, step, 0)


class Place:
    def __init__(self, n):
        self.n = n
        self.A, self.B = plane(n)
        self.me = lax.axis_index("tensor")
        self.a = self.me // self.B
        self.b = self.me % self.B

    def across(self, o):
        return (self.b + o) % self.B

    def peer(self, a, b):
        return {"tensor": a * self.B + b}


def greet(place, dp_peers=0):
    barrier = pltpu.get_barrier_semaphore()
    pc = place

    def signal(device):
        pl.semaphore_signal(barrier, inc=1, device_id=device, device_id_type=MESH)

    @pl.when(pc.a > 0)
    def _():
        signal(pc.peer(pc.a - 1, pc.b))

    @pl.when(pc.a < pc.A - 1)
    def _():
        signal(pc.peer(pc.a + 1, pc.b))

    for o in range(1, pc.B):
        signal(pc.peer(pc.a, pc.across(o)))
    dp = lax.axis_index("dp")
    for o in range(1, dp_peers):
        signal({"dp": (dp + o) % dp_peers})
    count = pc.B - 1 + max(dp_peers - 1, 0)
    ends = jnp.where((pc.a == 0) | (pc.a == pc.A - 1), 1, 2)
    pl.semaphore_wait(barrier, count + ends)


def remote(src, dst, send, recv, device):
    return pltpu.make_async_remote_copy(
        src_ref=src, dst_ref=dst, send_sem=send, recv_sem=recv, device_id=device, device_id_type=MESH
    )


class Gather:
    def __init__(self, place, buf, recv, up, down, side):
        self.pc, self.buf, self.recv, self.up, self.down, self.side = place, buf, recv, up, down, side

    def copy_up(self, a0):
        pc = self.pc
        blk = a0 * pc.B + pc.b
        return remote(self.buf.at[blk], self.buf.at[blk], self.up.at[a0], self.recv.at[blk],
                      pc.peer(jnp.minimum(pc.a + 1, pc.A - 1), pc.b))

    def copy_down(self, a0):
        pc = self.pc
        blk = a0 * pc.B + pc.b
        return remote(self.buf.at[blk], self.buf.at[blk], self.down.at[a0], self.recv.at[blk],
                      pc.peer(jnp.maximum(pc.a - 1, 0), pc.b))

    def copy_side(self, a0, o):
        pc = self.pc
        blk = a0 * pc.B + pc.b
        return remote(self.buf.at[blk], self.buf.at[blk], self.side.at[a0, o - 1], self.recv.at[blk],
                      pc.peer(pc.a, pc.across(o)))

    def arrived(self, blk):
        pc = self.pc
        remote(self.buf.at[blk], self.buf.at[blk], self.up.at[0], self.recv.at[blk],
               pc.peer(pc.a, pc.across(1))).wait_recv()

    def start(self):
        pc = self.pc

        @pl.when(pc.a < pc.A - 1)
        def _():
            self.copy_up(pc.a).start()

        @pl.when(pc.a > 0)
        def _():
            self.copy_down(pc.a).start()

        for o in range(1, pc.B):
            self.copy_side(pc.a, o).start()

    def round(self, r, use=None):
        pc = self.pc

        @pl.when(pc.a - r >= 0)
        def _():
            a0 = pc.a - r
            self.arrived(a0 * pc.B + pc.b)

            @pl.when(pc.a < pc.A - 1)
            def _():
                self.copy_up(a0).start()

            for o in range(1, pc.B):
                self.copy_side(a0, o).start()

        @pl.when(pc.a + r < pc.A)
        def _():
            a0 = pc.a + r
            self.arrived(a0 * pc.B + pc.b)

            @pl.when(pc.a > 0)
            def _():
                self.copy_down(a0).start()

            for o in range(1, pc.B):
                self.copy_side(a0, o).start()

    def rounds(self):
        for r in range(1, self.pc.A):
            self.round(r)

    def finish(self):
        pc = self.pc
        for a0 in range(pc.A):
            for o in range(1, pc.B):
                self.arrived(a0 * pc.B + pc.across(o))
        for a0 in range(pc.A):
            for o in range(1, pc.B):
                self.copy_side(a0, o).wait_send()

            @pl.when((pc.a >= a0) & (pc.a < pc.A - 1))
            def _():
                self.copy_up(a0).wait_send()

            @pl.when((pc.a <= a0) & (pc.a > 0))
            def _():
                self.copy_down(a0).wait_send()


def gather_sems(n):
    A, B = plane(n)
    dma = pltpu.SemaphoreType.DMA
    return [dma((n,)), dma((A,)), dma((A,)), dma((A, max(B - 1, 1)))]


class Scatter:
    def __init__(self, place, term, side_in, up_in, down_in, up_out, down_out,
                 side_send, side_recv, up_send, up_recv, down_send, down_recv):
        self.pc, self.term = place, term
        self.side_in, self.up_in, self.down_in = side_in, up_in, down_in
        self.up_out, self.down_out = up_out, down_out
        self.side_send, self.side_recv = side_send, side_recv
        self.up_send, self.up_recv = up_send, up_recv
        self.down_send, self.down_recv = down_send, down_recv
        self.rows = term.shape[1]

    def copy_side(self, a0, o):
        pc = self.pc
        return remote(self.term.at[a0 * pc.B + pc.across(o)], self.side_in.at[a0, o - 1],
                      self.side_send.at[a0, o - 1], self.side_recv.at[a0, o - 1],
                      pc.peer(pc.a, pc.across(o)))

    def copy_up(self, d):
        pc = self.pc
        return remote(self.up_out.at[d], self.up_in.at[d], self.up_send.at[d], self.up_recv.at[d],
                      pc.peer(jnp.minimum(pc.a + 1, pc.A - 1), pc.b))

    def copy_down(self, d):
        pc = self.pc
        return remote(self.down_out.at[d], self.down_in.at[d], self.down_send.at[d], self.down_recv.at[d],
                      pc.peer(jnp.maximum(pc.a - 1, 0), pc.b))

    def start(self):
        pc = self.pc
        for r in range(pc.A - 1, 0, -1):
            for sign in (1, -1):
                d = pc.a + sign * r

                @pl.when((d >= 0) & (d < pc.A))
                def _():
                    for o in range(1, pc.B):
                        self.copy_side(d, o).start()
        for o in range(1, pc.B):
            self.copy_side(pc.a, o).start()

    def local(self, d, rows):
        pc = self.pc
        total = self.term[d * pc.B + pc.b, rows, :].astype(jnp.float32)
        for o in range(1, pc.B):
            total = total + self.side_in[d, o - 1, rows, :].astype(jnp.float32)
        return total

    def forward(self, d, first, arrived, out, make_copy):
        pc = self.pc
        for o in range(1, pc.B):
            self.copy_side(d, o).wait_recv()

        @pl.when(first)
        def _():
            def body(rows):
                out[d, rows, :] = self.local(d, rows).astype(jnp.bfloat16)

            row_loop(self.rows, body)

        @pl.when(jnp.logical_not(first))
        def _():
            make_copy(d).wait_recv()

            def body(rows):
                out[d, rows, :] = (self.local(d, rows) + arrived[d, rows, :].astype(jnp.float32)).astype(jnp.bfloat16)

            row_loop(self.rows, body)

        make_copy(d).start()

    def rounds(self):
        pc = self.pc
        for r in range(pc.A - 1, 0, -1):
            @pl.when(pc.a + r < pc.A)
            def _():
                self.forward(pc.a + r, pc.a == 0, self.up_in, self.up_out, self.copy_up)

            @pl.when(pc.a - r >= 0)
            def _():
                self.forward(pc.a - r, pc.a == pc.A - 1, self.down_in, self.down_out, self.copy_down)

    def result(self, use):
        pc = self.pc
        for o in range(1, pc.B):
            self.copy_side(pc.a, o).wait_recv()

        @pl.when(pc.a == 0)
        def _():
            self.copy_down(pc.a).wait_recv()
            row_loop(self.rows, lambda rows: use(
                rows, self.local(pc.a, rows) + self.down_in[pc.a, rows, :].astype(jnp.float32)))

        @pl.when(pc.a == pc.A - 1)
        def _():
            self.copy_up(pc.a).wait_recv()
            row_loop(self.rows, lambda rows: use(
                rows, self.local(pc.a, rows) + self.up_in[pc.a, rows, :].astype(jnp.float32)))

        @pl.when((pc.a > 0) & (pc.a < pc.A - 1))
        def _():
            self.copy_up(pc.a).wait_recv()
            self.copy_down(pc.a).wait_recv()
            row_loop(self.rows, lambda rows: use(
                rows, self.local(pc.a, rows) + self.up_in[pc.a, rows, :].astype(jnp.float32)
                + self.down_in[pc.a, rows, :].astype(jnp.float32)))

    def finish(self):
        pc = self.pc
        for d in range(pc.A):
            for o in range(1, pc.B):
                self.copy_side(d, o).wait_send()

            @pl.when(pc.a < d)
            def _():
                self.copy_up(d).wait_send()

            @pl.when(pc.a > d)
            def _():
                self.copy_down(d).wait_send()


def scatter_scratch(n, rows, width):
    A, B = plane(n)
    dma = pltpu.SemaphoreType.DMA
    side = max(B - 1, 1)
    buf = pltpu.VMEM((A, rows, width), jnp.bfloat16)
    return [pltpu.VMEM((A, side, rows, width), jnp.bfloat16), buf, buf, buf, buf,
            dma((A, side)), dma((A, side)), dma((A,)), dma((A,)), dma((A,)), dma((A,))]


def enter_kernel(n, ndp, hidden, gain, prefix, owners, normed, cached,
                 from_dp, dp_send, dp_recv, *sems):
    pc = Place(n)
    dp = lax.axis_index("dp")
    greet(pc, ndp)

    def to_dp(o):
        return remote(prefix.at[0], from_dp.at[dp], dp_send.at[o - 1], dp_recv.at[dp],
                      {"dp": (dp + o) % ndp})

    for o in range(1, ndp):
        to_dp(o).start()
    gains = gain[...].astype(jnp.float32)

    def first(rows):
        normed[pc.me, rows, :] = norm_rows(hidden[rows, :].astype(jnp.float32), gains)

    row_loop(hidden.shape[0], first)
    tokens = Gather(pc, normed, *sems[:4])
    tokens.start()
    from_dp[dp] = prefix[0]
    tokens.rounds()
    for o in range(1, ndp):
        src = (dp + o) % ndp
        remote(prefix.at[0], from_dp.at[src], dp_send.at[0], dp_recv.at[src],
               {"dp": (dp + 1) % ndp}).wait_recv()
    cached[pc.me] = from_dp[owners[dp]]
    keys = Gather(pc, cached, *sems[4:])
    keys.start()
    keys.rounds()
    tokens.finish()
    keys.finish()
    for o in range(1, ndp):
        to_dp(o).wait_send()


def middle_kernel(n, term, hidden, gain, attended, middle, normed, *scratch):
    pc = Place(n)
    greet(pc)
    scatter = Scatter(pc, term, *scratch[:11])
    scatter.start()
    scatter.rounds()
    gains = gain[...].astype(jnp.float32)

    def use(rows, total):
        out = total.astype(jnp.bfloat16)
        attended[rows, :] = out
        mid = (hidden[rows, :].astype(jnp.float32) + out.astype(jnp.float32)).astype(jnp.bfloat16)
        middle[rows, :] = mid
        normed[pc.me, rows, :] = norm_rows(mid.astype(jnp.float32), gains)

    scatter.result(use)
    gather = Gather(pc, normed, *scratch[11:])
    gather.start()
    gather.rounds()
    scatter.finish()
    gather.finish()


def leave_kernel(n, term, middle, out, *scratch):
    pc = Place(n)
    greet(pc)
    scatter = Scatter(pc, term, *scratch)
    scatter.start()
    scatter.rounds()

    def use(rows, total):
        out[rows, :] = (middle[rows, :].astype(jnp.float32) + total).astype(jnp.bfloat16)

    scatter.result(use)
    scatter.finish()


VM = pl.BlockSpec(memory_space=pltpu.VMEM)


def params(cid):
    return pltpu.CompilerParams(collective_id=cid, has_side_effects=True, vmem_limit_bytes=48 << 20)


def attend_block(state_in, queries, key_rows, value_rows, allowed):
    running, totals, weighted = state_in
    scores = jnp.einsum("htd,kd->htk", queries, key_rows, preferred_element_type=jnp.float32)
    if allowed is not None:
        scores = jnp.where(allowed[None], scores, -jnp.inf)
    new_top = jnp.maximum(running, jnp.max(scores, axis=-1))
    factor = jnp.exp(running - new_top)
    probs = jnp.exp(scores - new_top[..., None])
    totals = totals * factor + jnp.sum(probs, axis=-1)
    probs_b = probs.astype(jnp.bfloat16)
    weighted = weighted * factor[..., None] + jnp.einsum(
        "htk,kd->htd", probs_b, value_rows, preferred_element_type=jnp.float32
    )
    return (new_top, totals, weighted)


def local(n, ndp, hidden_in, norm1_gain, norm2_gain, w_query, w_keyval, w_out, w_fc, w_proj,
          prefix_kv, owner_ids, segment_ids):
    rows, width = hidden_in.shape
    head_size = w_keyval.shape[1] // 2
    query_cols = w_query.shape[1]
    heads_here = query_cols // head_size
    row_len = segment_ids.shape[1]
    span = prefix_kv.shape[1]
    q_scale = 1.0 / math.sqrt(head_size)
    bf = jnp.bfloat16
    dma = pltpu.SemaphoreType.DMA
    normed, cached = pl.pallas_call(
        functools.partial(enter_kernel, n, ndp),
        out_shape=(jax.ShapeDtypeStruct((n, rows, width), bf),
                   jax.ShapeDtypeStruct((n, span, 2 * head_size), bf)),
        in_specs=[VM, VM, VM, pl.BlockSpec(memory_space=pltpu.SMEM)],
        out_specs=(VM, VM),
        scratch_shapes=[pltpu.VMEM((ndp, span, 2 * head_size), bf), dma((ndp,)), dma((ndp,))]
        + gather_sems(n) + gather_sems(n),
        compiler_params=params(1),
        name="enter",
    )(hidden_in, norm1_gain.reshape(1, -1), prefix_kv, owner_ids)
    normed = normed.reshape(row_len, width)
    fragment = cached.reshape(n * span, 2 * head_size)
    w_joint = jnp.concatenate([w_query, w_keyval], axis=1)
    col_scale = jnp.concatenate(
        [jnp.full((query_cols,), q_scale, jnp.float32), jnp.ones((2 * head_size,), jnp.float32)]
    )
    projected = (jnp.dot(normed, w_joint, preferred_element_type=jnp.float32) * col_scale).astype(bf)
    queries = projected[:, :query_cols].reshape(row_len, heads_here, head_size).transpose(1, 0, 2)
    suffix_keys = projected[:, query_cols : query_cols + head_size]
    suffix_values = projected[:, query_cols + head_size :]
    request_ids = segment_ids[0]
    positions = jnp.arange(row_len, dtype=jnp.int32)
    allowed = (positions[None, :] <= positions[:, None]) & (
        request_ids[None, :] == request_ids[:, None]
    )
    state = (
        jnp.full((heads_here, row_len), -jnp.inf, jnp.float32),
        jnp.zeros((heads_here, row_len), jnp.float32),
        jnp.zeros((heads_here, row_len, head_size), jnp.float32),
    )
    state = attend_block(state, queries, suffix_keys, suffix_values, allowed)
    for row_begin in range(0, fragment.shape[0], 1024):
        block_rows = fragment[row_begin : row_begin + 1024]
        state = attend_block(state, queries, block_rows[:, :head_size], block_rows[:, head_size:], None)
    running, totals, weighted = state
    attn_heads = (
        (weighted / totals[..., None]).astype(bf).transpose(1, 0, 2).reshape(row_len, query_cols)
    )
    term = jnp.dot(attn_heads, w_out, preferred_element_type=jnp.float32).astype(bf)
    own = jax.ShapeDtypeStruct((rows, width), bf)
    attended, middle, normed2 = pl.pallas_call(
        functools.partial(middle_kernel, n),
        out_shape=(own, own, jax.ShapeDtypeStruct((n, rows, width), bf)),
        in_specs=[VM] * 3,
        out_specs=(VM, VM, VM),
        scratch_shapes=scatter_scratch(n, rows, width) + gather_sems(n),
        compiler_params=params(2),
        name="middle",
    )(term.reshape(n, rows, width), hidden_in, norm2_gain.reshape(1, -1))
    hidden_act = jax.nn.gelu(
        jnp.dot(normed2.reshape(row_len, width), w_fc, preferred_element_type=jnp.float32),
        approximate=True,
    ).astype(bf)
    term = jnp.dot(hidden_act, w_proj, preferred_element_type=jnp.float32).astype(bf)
    layer_out = pl.pallas_call(
        functools.partial(leave_kernel, n),
        out_shape=own,
        in_specs=[VM] * 2,
        out_specs=VM,
        scratch_shapes=scatter_scratch(n, rows, width),
        compiler_params=params(3),
        name="leave",
    )(term.reshape(n, rows, width), middle)
    return (layer_out, attended)


def solution(mesh):
    return jax.shard_map(
        functools.partial(local, mesh.shape["tensor"], mesh.shape["dp"]),
        mesh=mesh,
        in_specs=(
            P(("dp", "tensor"), None),
            P(),
            P(),
            P(None, "tensor"),
            P(),
            P("tensor", None),
            P(None, "tensor"),
            P("tensor", None),
            P("dp", "tensor", None),
            P(),
            P("dp", None),
        ),
        out_specs=(P(("dp", "tensor"), None), P(("dp", "tensor"), None)),
        check_vma=False,
    )
```

time: 393 us -> 233 us (0.59)
  waiting for transfers between devices: 323 us -> 0 us
  Pallas kernels: 0 us -> 182 us
  between operations: 14.4 us -> 0.83 us
  other arithmetic: 19.4 us -> 6.37 us
  local copies, waits for them, and re-layouts: 3.65 us -> 10.8 us
    pallas_call x0 -> x3, Pallas kernels: none -> 182 us  [the longest x1 79.3 us: local(): pl.pallas_call(functools.partial(middle_kernel, n), out_shape=(own, own,...]
    all_gather x4 -> x0, waiting for transfers between devices: 176 us -> none  [the longest x1 59.8 us: local(): lax.all_gather(normed, 'tensor', axis=0, tiled=True)]
    reduce_scatter x2 -> x0, waiting for transfers between devices: 146 us -> none  [local(): lax.psum_scatter(term.astype(jnp.bfloat16).astype(jnp.float32).astype(jnp...]
    reduce_sum x5 -> x0, other arithmetic: 6.13 us -> none  [the longest x2 2.36 us: layer_norm(): centre = jnp.mean(widened, axis=-1, keepdims=True)]
    unnamed x18 -> x22, local copies, waits for them, and re-layouts: 2.16 us -> 7.85 us
    convert_element_type x5 -> x0, other arithmetic: 5.57 us -> none  [the longest x2 3.04 us: layer_norm(): (centred * lax.rsqrt(variance + 1e-05) * scales.astype(jnp.float32)).asty...]
  transfers between devices with their start and end apart: 6 -> 0, of which waited for: 6 -> 0; matrix products, arithmetic and copies ran while one was open for 4% -> 0% of each run, Pallas kernels for 0% -> 0%
where the time goes in v1:
time: 233 us; the launch traced here: 232 us
  Pallas kernels  182 us (78%)
  matrix products  32.4 us (14%)
  local copies, waits for them, and re-layouts  10.8 us (5%)
  other arithmetic  6.37 us (3%)
    pallas_call x1, Pallas kernels, local(): pl.pallas_call(functools.partial(middle_kernel, n), out_shape=(own, own,...  79.3 us
    pallas_call x1, Pallas kernels, local(): pl.pallas_call(functools.partial(enter_kernel, n, ndp), out_shape=(jax.Sh...  67.6 us
    pallas_call x1, Pallas kernels, local(): pl.pallas_call(functools.partial(leave_kernel, n), out_shape=own, in_spec...  35 us
    dot_general x1, matrix products, local(): jnp.dot(hidden_act, w_proj, preferred_element_type=jnp.float32).astype(bf)  12.5 us
    unnamed x22, local copies, waits for them, and re-layouts  7.85 us
    dot_general x5, matrix products, attend_block(): jnp.einsum('htk,kd->htd', probs_b, value_rows, preferred_element_type=jnp...  7.53 us
    dot_general x5, matrix products, attend_block(): jnp.einsum('htd,kd->htk', queries, key_rows, preferred_element_type=jnp.f...  6.2 us
    reduce_sum x3, other arithmetic, attend_block(): totals = totals * factor + jnp.sum(probs, axis=-1)  5.93 us

profile of v1, /device:TPU:0, one launch (start us, length us, event | category | flops | bytes accessed | tf_op | source)
XLA Modules:
  0.0 232.4 jit_solution(16020763386540566531)
XLA Ops:
  1.4 1.0 copy-done.2
  2.4 0.9 copy-done.4
  4.0 67.6 %enter.1 = (bf16[8,96,2048]{2,1,0:T(8,128)(2,1)S(1)}, bf16[8,512,256]{2,1,0:T(8,128)(2,1)S(1)}) custom-call(bf16[96,2048]{1,0:T(8,128)(2,1)S(1)} %copy-done.2, bf16[1,2048]{1,0:T(2,128)(2,1)S(1)} %reshape.179.gain, bf16[1,512,256]{2,1,0:T(8,128)(2,1)S(1)} %copy-done.4, s32[4]{0:T(128)S(1)} %copy-done.5), custom_call_target="tpu_custom_call" | custom-call | tf_op jit(solution)/shard_map/enter/pallas_call | solution.py:414
  71.6 3.5 %multiply_convert_fusion = bf16[768,512]{0,1:T(8,128)(2,1)S(1)} fusion(bf16[768,2048]{1,0:T(8,128)(2,1)S(1)} %bitcast.205, bf16[2048,256]{1,0:T(8,128)(2,1)} %param.15, bf16[2048,256]{1,0:T(8,128)(2,1)} %param.14, f32[512]{0:T(512)} %constant.8.clone.1), kind=kOutput, calls=%fused_computation.49 | convolution fusion | flops 1615593472 | bytes 6031360 | tf_op jit(solution)/shard_map/dot_general | solution.py:431
  76.2 1.2 copy.13
  77.8 1.9 select_reduce_fusion
  79.9 1.1 fusion.124
  80.9 1.1 fusion.125
  82.0 1.1 fusion.126
  83.1 1.1 fusion.123
  84.2 2.4 %fusion = (f32[2,768]{1,0:T(2,128)S(1)}, f32[2,768]{1,0:T(2,128)S(1)}) fusion(f32[2,768,1024]{2,1,0:T(8,128)S(1)} %get-tuple-element.35, f32[2,768]{1,0:T(2,128)S(1)} %get-tuple-element.20, f32[2,768,1024]{2,1,0:T(8,128)S(1)} %get-tuple-element.31, f32[2,768]{1,0:T(2,128)S(1)} %get-tuple-element.19), kind=kLoop, calls=%fused_computation.4 | loop fusion | flops 6288384 | bytes 12607488 | tf_op jit(solution)/shard_map/reduce_sum | solution.py:395
  86.6 2.6 %fusion.4 = (f32[2,768]{1,0:T(2,128)S(1)}, f32[2,768]{1,0:T(2,128)S(1)}) fusion(f32[2,768,1024]{2,1,0:T(8,128)S(1)} %get-tuple-element.29, f32[2,768]{1,0:T(2,128)S(1)} %get-tuple-element.18, f32[2,768,1024]{2,1,0:T(8,128)S(1)} %get-tuple-element.27, f32[2,768]{1,0:T(2,128)S(1)} %get-tuple-element.17), kind=kLoop, calls=%fused_computation.8 | loop fusion | flops 6288384 | bytes 12607488 | tf_op jit(solution)/shard_map/reduce_sum | solution.py:395
  89.2 0.9 fusion.8
  90.2 1.3 fusion.50
  91.4 1.3 fusion.53
  92.7 1.3 fusion.56
  94.0 1.3 fusion.59
  95.2 2.5 %fusion.92 = bf16[768,2,128]{0,2,1:T(8,128)(2,1)S(1)} fusion(f32[768,2,128]{0,2,1:T(8,128)S(1)} %fusion.59, f32[768,2,128]{0,2,1:T(8,128)S(1)} %fusion.56, f32[768,2,128]{0,2,1:T(8,128)S(1)} %fusion.53, f32[768,2,128]{0,2,1:T(8,128)S(1)} %fusion.50, f32[2,768,768]{1,2,0:T(8,128)S(1)} %get-tuple-element.33, f32[2,768]{1,0:T(2,128)S(1)} %get-tuple-element.32, ...), kind=kOutput, calls=%fused_computation.65 | convolution fusion | flops 307691520 | bytes 9086976 | tf_op jit(solution)/shard_map/htk,kd->htd/dot_general | solution.py:397
  97.8 2.7 %convolution_convert_fusion.1 = bf16[768,2048]{1,0:T(8,128)(2,1)} fusion(bf16[768,256]{0,1:T(8,128)(2,1)S(1)} %bitcast.216, bf16[256,2048]{1,0:T(8,128)(2,1)S(1)} %copy-done), kind=kOutput, calls=%fused_computation.18 | convolution fusion | flops 806879232 | bytes 4587520 | tf_op jit(solution)/shard_map/dot_general | solution.py:453
  100.5 79.3 %middle.1 = (bf16[96,2048]{1,0:T(8,128)(2,1)S(1)}, bf16[96,2048]{1,0:T(8,128)(2,1)S(1)}, bf16[8,96,2048]{2,1,0:T(8,128)(2,1)S(1)}) custom-call(bf16[8,96,2048]{2,1,0:T(8,128)(2,1)} %bitcast.206, bf16[96,2048]{1,0:T(8,128)(2,1)S(1)} %copy-done.3, bf16[1,2048]{1,0:T(2,128)(2,1)S(1)} %reshape.184.gain), custom_call_target="tpu_custom_call" | custom-call | tf_op jit(solution)/shard_map/middle/pallas_call | solution.py:455
  179.8 1.7 copy-done.6
  181.5 12.5 %convolution_convert_fusion = bf16[768,2048]{1,0:T(8,128)(2,1)} fusion(bf16[1024,2048]{1,0:T(8,128)(2,1)} %param.18, bf16[768,2048]{1,0:T(8,128)(2,1)} %bitcast.204, bf16[2048,1024]{1,0:T(8,128)(2,1)} %param.17), kind=kOutput, calls=%fused_computation.17 | convolution fusion | flops 6451101696 | bytes 14680064 | tf_op jit(solution)/shard_map/dot_general | solution.py:468
  194.0 1.9 copy-done.1
  195.9 35.0 %leave.1 = bf16[96,2048]{1,0:T(8,128)(2,1)S(1)} custom-call(bf16[8,96,2048]{2,1,0:T(8,128)(2,1)S(1)} %bitcast.203, bf16[96,2048]{1,0:T(8,128)(2,1)S(1)} %get-tuple-element.10.middle), custom_call_target="tpu_custom_call" | custom-call | tf_op jit(solution)/shard_map/leave/pallas_call | solution.py:469
  (26 shorter events, 4.6 us)
Async XLA Ops:
  0.6 97.1 %copy-start = (bf16[256,2048]{1,0:T(8,128)(2,1)S(1)}, bf16[256,2048]{1,0:T(8,128)(2,1)}, u32[]{:S(2)}) copy-start(bf16[256,2048]{1,0:T(8,128)(2,1)} %param.16) | copy-start | bytes 3145732
  1.4 1.0 copy-start.2
  2.4 0.9 copy-start.4
  3.4 0.7 copy-start.5
  71.6 5.8 %copy-start.9 = (s32[1,768]{1,0:T(1,128)S(1)}, s32[1,768]{1,0:T(1,128)}, u32[]{:S(2)}) copy-start(s32[1,768]{1,0:T(1,128)} %param.21) | copy-start | bytes 9220
  75.2 1.0 copy-start.7
  97.7 2.7 %copy-start.8 = (bf16[2048]{0:T(1024)(128)(2,1)S(1)}, bf16[2048]{0:T(1024)(128)(2,1)}, u32[]{:S(2)}) copy-start(bf16[2048]{0:T(1024)(128)(2,1)} %param.13) | copy-start | bytes 12292
  97.7 2.7 %copy-start.3 = (bf16[96,2048]{1,0:T(8,128)(2,1)S(1)}, bf16[96,2048]{1,0:T(8,128)(2,1)}, u32[]{:S(2)}) copy-start(bf16[96,2048]{1,0:T(8,128)(2,1)} %hidden.3) | copy-start | bytes 1179652
  179.8 1.7 copy-start.6
  194.0 1.9 copy-start.1

commit v2 on v1

--- a/solution.py
+++ b/solution.py
@@ -45,6 +45,14 @@
 
     def peer(self, a, b):
         return {"tensor": a * self.B + b}
+
+    def far(self, k):
+        found = 0
+        for a in range(self.A):
+            order = sorted(range(self.A), key=lambda d: (-abs(d - a), -d))
+            for i, d in enumerate(order):
+                found = found + jnp.where((self.a == a) & (k == i), d, 0)
+        return found
 
 
 def greet(place, dp_peers=0):
@@ -150,11 +158,12 @@
         for r in range(1, self.pc.A):
             self.round(r)
 
+    def pair_arrived(self, a0):
+        for o in range(1, self.pc.B):
+            self.arrived(a0 * self.pc.B + self.pc.across(o))
+
     def finish(self):
         pc = self.pc
-        for a0 in range(pc.A):
-            for o in range(1, pc.B):
-                self.arrived(a0 * pc.B + pc.across(o))
         for a0 in range(pc.A):
             for o in range(1, pc.B):
                 self.copy_side(a0, o).wait_send()
@@ -201,18 +210,9 @@
         return remote(self.down_out.at[d], self.down_in.at[d], self.down_send.at[d], self.down_recv.at[d],
                       pc.peer(jnp.maximum(pc.a - 1, 0), pc.b))
 
-    def start(self):
-        pc = self.pc
-        for r in range(pc.A - 1, 0, -1):
-            for sign in (1, -1):
-                d = pc.a + sign * r
-
-                @pl.when((d >= 0) & (d < pc.A))
-                def _():
-                    for o in range(1, pc.B):
-                        self.copy_side(d, o).start()
-        for o in range(1, pc.B):
-            self.copy_side(pc.a, o).start()
+    def start(self, d):
+        for o in range(1, self.pc.B):
+            self.copy_side(d, o).start()
 
     def local(self, d, rows):
         pc = self.pc
@@ -244,16 +244,41 @@
 
         make_copy(d).start()
 
-    def rounds(self):
-        pc = self.pc
-        for r in range(pc.A - 1, 0, -1):
-            @pl.when(pc.a + r < pc.A)
-            def _():
-                self.forward(pc.a + r, pc.a == 0, self.up_in, self.up_out, self.copy_up)
-
-            @pl.when(pc.a - r >= 0)
-            def _():
-                self.forward(pc.a - r, pc.a == pc.A - 1, self.down_in, self.down_out, self.copy_down)
+    def pass_on(self, d):
+        pc = self.pc
+
+        @pl.when(d > pc.a)
+        def _():
+            self.forward(d, pc.a == 0, self.up_in, self.up_out, self.copy_up)
+
+        @pl.when(d < pc.a)
+        def _():
+            self.forward(d, pc.a == pc.A - 1, self.down_in, self.down_out, self.copy_down)
+
+    def run(self, compute):
+        pc = self.pc
+        end = (pc.a == 0) | (pc.a == pc.A - 1)
+
+        def step(k, carry):
+            d = pc.far(k)
+            compute(d)
+            self.start(d)
+
+            @pl.when((k >= 1) & end)
+            def _():
+                self.pass_on(pc.far(k - 1))
+
+            return carry
+
+        lax.fori_loop(0, pc.A, step, 0)
+
+        @pl.when(jnp.logical_not(end))
+        def _():
+            def late(k, carry):
+                self.pass_on(pc.far(k))
+                return carry
+
+            lax.fori_loop(0, pc.A - 1, late, 0)
 
     def result(self, use):
         pc = self.pc
@@ -304,28 +329,46 @@
             dma((A, side)), dma((A, side)), dma((A,)), dma((A,)), dma((A,)), dma((A,))]
 
 
-def enter_kernel(n, ndp, hidden, gain, prefix, owners, normed, cached,
-                 from_dp, dp_send, dp_recv, *sems):
+def enter_kernel(n, ndp, q_scale, hidden, gain, prefix, w_query, w_keyval, owners, projected, cached,
+                 normed, from_dp, dp_send, dp_recv, *sems):
     pc = Place(n)
     dp = lax.axis_index("dp")
     greet(pc, ndp)
+    rows, width = hidden.shape
+    slab = pc.B * rows
+    query_cols = w_query.shape[1]
 
     def to_dp(o):
         return remote(prefix.at[0], from_dp.at[dp], dp_send.at[o - 1], dp_recv.at[dp],
                       {"dp": (dp + o) % ndp})
 
+    gains = gain[...].astype(jnp.float32)
+
+    def first(part):
+        normed[pc.me, part, :] = norm_rows(hidden[part, :].astype(jnp.float32), gains)
+
+    row_loop(rows, first)
+    tokens = Gather(pc, normed, *sems[:4])
+    tokens.start()
     for o in range(1, ndp):
         to_dp(o).start()
-    gains = gain[...].astype(jnp.float32)
-
-    def first(rows):
-        normed[pc.me, rows, :] = norm_rows(hidden[rows, :].astype(jnp.float32), gains)
-
-    row_loop(hidden.shape[0], first)
-    tokens = Gather(pc, normed, *sems[:4])
-    tokens.start()
     from_dp[dp] = prefix[0]
-    tokens.rounds()
+
+    def project(d):
+        tokens.pair_arrived(d)
+        left = normed[pl.ds(d * pc.B, pc.B)].reshape(slab, width)
+        here = pl.ds(pl.multiple_of(d * slab, slab), slab)
+        projected[here, :query_cols] = (
+            jnp.dot(left, w_query[...], preferred_element_type=jnp.float32) * q_scale
+        ).astype(jnp.bfloat16)
+        projected[here, query_cols:] = jnp.dot(
+            left, w_keyval[...], preferred_element_type=jnp.float32
+        ).astype(jnp.bfloat16)
+
+    for r in range(1, pc.A):
+        tokens.round(r)
+        if r < pc.A - 1:
+            project(pc.far(pc.A - r))
     for o in range(1, ndp):
         src = (dp + o) % ndp
         remote(prefix.at[0], from_dp.at[src], dp_send.at[0], dp_recv.at[src],
@@ -333,71 +376,143 @@
     cached[pc.me] = from_dp[owners[dp]]
     keys = Gather(pc, cached, *sems[4:])
     keys.start()
-    keys.rounds()
+    project(pc.far(1))
+    keys.round(1)
+    project(pc.far(0))
+    for r in range(2, pc.A):
+        keys.round(r)
+    for a0 in range(pc.A):
+        keys.pair_arrived(a0)
     tokens.finish()
     keys.finish()
     for o in range(1, ndp):
         to_dp(o).wait_send()
 
 
-def middle_kernel(n, term, hidden, gain, attended, middle, normed, *scratch):
+def core_kernel(n, heads, projected, cached, seg_rows, seg_cols, w_out, hidden, gain, w_fc_hbm, w_proj_hbm,
+                attended, layer_out, *scratch):
     pc = Place(n)
+    w_fc, w_proj, fc_sem, proj_sem, term, term2, normed, middle, act = scratch[:9]
     greet(pc)
-    scatter = Scatter(pc, term, *scratch[:11])
-    scatter.start()
-    scatter.rounds()
+    load_fc = pltpu.make_async_copy(w_fc_hbm, w_fc, fc_sem)
+    load_proj = pltpu.make_async_copy(w_proj_hbm, w_proj, proj_sem)
+    load_fc.start()
+    load_proj.start()
+    rows, width = hidden.shape
+    slab = pc.B * rows
+    row_len = projected.shape[0]
+    head = cached.shape[1] // 2
+    q_cols = heads * head
+    span = min(1024, cached.shape[0])
+
+    def block(q, state, keys, values, allowed):
+        top, total, weighted = state
+        scores = lax.dot_general(q, keys, (((1,), (1,)), ((), ())), preferred_element_type=jnp.float32)
+        if allowed is not None:
+            scores = jnp.where(allowed[None], scores.reshape(heads, slab, -1), -jnp.inf)
+            scores = scores.reshape(heads * slab, -1)
+        new_top = jnp.maximum(top, jnp.max(scores, axis=-1, keepdims=True))
+        factor = jnp.exp(top - new_top)
+        probs = jnp.exp(scores - new_top)
+        total = total * factor + jnp.sum(probs, axis=-1, keepdims=True)
+        weighted = weighted * factor + jnp.dot(
+            probs.astype(jnp.bfloat16), values, preferred_element_type=jnp.float32
+        )
+        return new_top, total, weighted
+
+    def emit(left, weights, cols, target, d):
+        wide = min(512, width)
+
+        def column(c, carry):
+            here = pl.ds(pl.multiple_of(c * wide, wide), wide)
+            out = jnp.dot(left, weights[:, here], preferred_element_type=jnp.float32)
+            target[pl.ds(d * pc.B, pc.B), :, here] = out.astype(jnp.bfloat16).reshape(pc.B, rows, wide)
+            return carry
+
+        lax.fori_loop(0, width // wide, column, 0)
+
+    def attend(d):
+        here = pl.ds(pl.multiple_of(d * slab, slab), slab)
+        q = jnp.concatenate([projected[here, h * head : (h + 1) * head] for h in range(heads)], axis=0)
+        state = (
+            jnp.full((heads * slab, 1), -jnp.inf, jnp.float32),
+            jnp.zeros((heads * slab, 1), jnp.float32),
+            jnp.zeros((heads * slab, head), jnp.float32),
+        )
+
+        def over(i, state):
+            part = pl.ds(pl.multiple_of(i * span, span), span)
+            return block(q, state, cached[part, :head], cached[part, head:], None)
+
+        state = lax.fori_loop(0, cached.shape[0] // span, over, state)
+        place = d * slab + lax.broadcasted_iota(jnp.int32, (slab, row_len), 0)
+        other = lax.broadcasted_iota(jnp.int32, (slab, row_len), 1)
+        allowed = (other <= place) & (seg_rows[here, :] == seg_cols[...])
+        top, total, weighted = block(
+            q, state, projected[:, q_cols : q_cols + head], projected[:, q_cols + head :], allowed
+        )
+        out = (weighted / total).astype(jnp.bfloat16)
+        left = jnp.concatenate([out[h * slab : (h + 1) * slab] for h in range(heads)], axis=1)
+        emit(left, w_out, q_cols, term, d)
+
+    scatter = Scatter(pc, term, *scratch[9:20])
+    scatter.run(attend)
     gains = gain[...].astype(jnp.float32)
 
-    def use(rows, total):
+    def use(part, total):
         out = total.astype(jnp.bfloat16)
-        attended[rows, :] = out
-        mid = (hidden[rows, :].astype(jnp.float32) + out.astype(jnp.float32)).astype(jnp.bfloat16)
-        middle[rows, :] = mid
-        normed[pc.me, rows, :] = norm_rows(mid.astype(jnp.float32), gains)
+        attended[part, :] = out
+        mid = (hidden[part, :].astype(jnp.float32) + out.astype(jnp.float32)).astype(jnp.bfloat16)
+        middle[part, :] = mid
+        normed[pc.me, part, :] = norm_rows(mid.astype(jnp.float32), gains)
 
     scatter.result(use)
-    gather = Gather(pc, normed, *scratch[11:])
+    gather = Gather(pc, normed, *scratch[20:24])
     gather.start()
-    gather.rounds()
+    load_fc.wait()
+    load_proj.wait()
+    units = w_fc.shape[1]
+    wide = min(256, units)
+
+    def expand(d):
+        gather.pair_arrived(d)
+        here = pl.ds(pl.multiple_of(d * slab, slab), slab)
+
+        def column(c, carry):
+            cols = pl.ds(pl.multiple_of(c * wide, wide), wide)
+            left = normed[pl.ds(d * pc.B, pc.B)].reshape(slab, width)
+            out = jnp.dot(left, w_fc[:, cols], preferred_element_type=jnp.float32)
+            act[here, cols] = jax.nn.gelu(out, approximate=True).astype(jnp.bfloat16)
+            return carry
+
+        lax.fori_loop(0, units // wide, column, 0)
+
+    for r in range(1, pc.A):
+        gather.round(r)
+        expand(pc.far(pc.A - r))
+    expand(pc.far(0))
+
+    def contract(d):
+        here = pl.ds(pl.multiple_of(d * slab, slab), slab)
+        emit(act[here, :], w_proj, units, term2, d)
+
+    scatter2 = Scatter(pc, term2, *scratch[24:])
+    scatter2.run(contract)
+
+    def last(part, total):
+        layer_out[part, :] = (middle[part, :].astype(jnp.float32) + total).astype(jnp.bfloat16)
+
+    scatter2.result(last)
     scatter.finish()
     gather.finish()
-
-
-def leave_kernel(n, term, middle, out, *scratch):
-    pc = Place(n)
-    greet(pc)
-    scatter = Scatter(pc, term, *scratch)
-    scatter.start()
-    scatter.rounds()
-
-    def use(rows, total):
-        out[rows, :] = (middle[rows, :].astype(jnp.float32) + total).astype(jnp.bfloat16)
-
-    scatter.result(use)
-    scatter.finish()
+    scatter2.finish()
 
 
 VM = pl.BlockSpec(memory_space=pltpu.VMEM)
 
 
 def params(cid):
-    return pltpu.CompilerParams(collective_id=cid, has_side_effects=True, vmem_limit_bytes=48 << 20)
-
-
-def attend_block(state_in, queries, key_rows, value_rows, allowed):
-    running, totals, weighted = state_in
-    scores = jnp.einsum("htd,kd->htk", queries, key_rows, preferred_element_type=jnp.float32)
-    if allowed is not None:
-        scores = jnp.where(allowed[None], scores, -jnp.inf)
-    new_top = jnp.maximum(running, jnp.max(scores, axis=-1))
-    factor = jnp.exp(running - new_top)
-    probs = jnp.exp(scores - new_top[..., None])
-    totals = totals * factor + jnp.sum(probs, axis=-1)
-    probs_b = probs.astype(jnp.bfloat16)
-    weighted = weighted * factor[..., None] + jnp.einsum(
-        "htk,kd->htd", probs_b, value_rows, preferred_element_type=jnp.float32
-    )
-    return (new_top, totals, weighted)
+    return pltpu.CompilerParams(collective_id=cid, has_side_effects=True, vmem_limit_bytes=60 << 20)
 
 
 def local(n, ndp, hidden_in, norm1_gain, norm2_gain, w_query, w_keyval, w_out, w_fc, w_proj,
@@ -411,70 +526,33 @@
     q_scale = 1.0 / math.sqrt(head_size)
     bf = jnp.bfloat16
     dma = pltpu.SemaphoreType.DMA
-    normed, cached = pl.pallas_call(
-        functools.partial(enter_kernel, n, ndp),
-        out_shape=(jax.ShapeDtypeStruct((n, rows, width), bf),
+    any_space = pl.BlockSpec(memory_space=pl.ANY)
+    projected, cached = pl.pallas_call(
+        functools.partial(enter_kernel, n, ndp, q_scale),
+        out_shape=(jax.ShapeDtypeStruct((row_len, query_cols + 2 * head_size), bf),
                    jax.ShapeDtypeStruct((n, span, 2 * head_size), bf)),
-        in_specs=[VM, VM, VM, pl.BlockSpec(memory_space=pltpu.SMEM)],
+        in_specs=[VM] * 5 + [pl.BlockSpec(memory_space=pltpu.SMEM)],
         out_specs=(VM, VM),
-        scratch_shapes=[pltpu.VMEM((ndp, span, 2 * head_size), bf), dma((ndp,)), dma((ndp,))]
-        + gather_sems(n) + gather_sems(n),
+        scratch_shapes=[pltpu.VMEM((n, rows, width), bf), pltpu.VMEM((ndp, span, 2 * head_size), bf),
+                        dma((ndp,)), dma((ndp,))] + gather_sems(n) + gather_sems(n),
         compiler_params=params(1),
         name="enter",
-    )(hidden_in, norm1_gain.reshape(1, -1), prefix_kv, owner_ids)
-    normed = normed.reshape(row_len, width)
-    fragment = cached.reshape(n * span, 2 * head_size)
-    w_joint = jnp.concatenate([w_query, w_keyval], axis=1)
-    col_scale = jnp.concatenate(
-        [jnp.full((query_cols,), q_scale, jnp.float32), jnp.ones((2 * head_size,), jnp.float32)]
-    )
-    projected = (jnp.dot(normed, w_joint, preferred_element_type=jnp.float32) * col_scale).astype(bf)
-    queries = projected[:, :query_cols].reshape(row_len, heads_here, head_size).transpose(1, 0, 2)
-    suffix_keys = projected[:, query_cols : query_cols + head_size]
-    suffix_values = projected[:, query_cols + head_size :]
-    request_ids = segment_ids[0]
-    positions = jnp.arange(row_len, dtype=jnp.int32)
-    allowed = (positions[None, :] <= positions[:, None]) & (
-        request_ids[None, :] == request_ids[:, None]
-    )
-    state = (
-        jnp.full((heads_here, row_len), -jnp.inf, jnp.float32),
-        jnp.zeros((heads_here, row_len), jnp.float32),
-        jnp.zeros((heads_here, row_len, head_size), jnp.float32),
-    )
-    state = attend_block(state, queries, suffix_keys, suffix_values, allowed)
-    for row_begin in range(0, fragment.shape[0], 1024):
-        block_rows = fragment[row_begin : row_begin + 1024]
-        state = attend_block(state, queries, block_rows[:, :head_size], block_rows[:, head_size:], None)
-    running, totals, weighted = state
-    attn_heads = (
-        (weighted / totals[..., None]).astype(bf).transpose(1, 0, 2).reshape(row_len, query_cols)
-    )
-    term = jnp.dot(attn_heads, w_out, preferred_element_type=jnp.float32).astype(bf)
+    )(hidden_in, norm1_gain.reshape(1, -1), prefix_kv, w_query, w_keyval, owner_ids)
     own = jax.ShapeDtypeStruct((rows, width), bf)
-    attended, middle, normed2 = pl.pallas_call(
-        functools.partial(middle_kernel, n),
-        out_shape=(own, own, jax.ShapeDtypeStruct((n, rows, width), bf)),
-        in_specs=[VM] * 3,
-        out_specs=(VM, VM, VM),
-        scratch_shapes=scatter_scratch(n, rows, width) + gather_sems(n),
+    terms = pltpu.VMEM((n, rows, width), bf)
+    attended, layer_out = pl.pallas_call(
+        functools.partial(core_kernel, n, heads_here),
+        out_shape=(own, own),
+        in_specs=[VM] * 7 + [any_space] * 2,
+        out_specs=(VM, VM),
+        scratch_shapes=[pltpu.VMEM(w_fc.shape, bf), pltpu.VMEM(w_proj.shape, bf), dma(()), dma(()),
+                        terms, terms, terms, pltpu.VMEM((rows, width), bf),
+                        pltpu.VMEM((row_len, w_fc.shape[1]), bf)]
+        + scatter_scratch(n, rows, width) + gather_sems(n) + scatter_scratch(n, rows, width),
         compiler_params=params(2),
-        name="middle",
-    )(term.reshape(n, rows, width), hidden_in, norm2_gain.reshape(1, -1))
-    hidden_act = jax.nn.gelu(
-        jnp.dot(normed2.reshape(row_len, width), w_fc, preferred_element_type=jnp.float32),
-        approximate=True,
-    ).astype(bf)
-    term = jnp.dot(hidden_act, w_proj, preferred_element_type=jnp.float32).astype(bf)
-    layer_out = pl.pallas_call(
-        functools.partial(leave_kernel, n),
-        out_shape=own,
-        in_specs=[VM] * 2,
-        out_specs=VM,
-        scratch_shapes=scatter_scratch(n, rows, width),
-        compiler_params=params(3),
-        name="leave",
-    )(term.reshape(n, rows, width), middle)
+        name="core",
+    )(projected, cached.reshape(n * span, 2 * head_size), segment_ids.reshape(-1, 1),
+      segment_ids.reshape(1, -1), w_out, hidden_in, norm2_gain.reshape(1, -1), w_fc, w_proj)
     return (layer_out, attended)
 
 

time: 233 us -> 206 us (0.88)
  matrix products: 32.4 us -> 0 us
  Pallas kernels: 182 us -> 197 us
  other arithmetic: 6.37 us -> 0 us
  local copies, waits for them, and re-layouts: 10.8 us -> 7.73 us
    dot_general x13 -> x0, matrix products: 32.4 us -> none  [the longest x1 12.5 us: local(): jnp.dot(hidden_act, w_proj, preferred_element_type=jnp.float32).astype(bf)]
    pallas_call x3 -> x2, Pallas kernels: 182 us -> 197 us  [the longest x1 126 us: local(): pl.pallas_call(functools.partial(core_kernel, n, heads_here), out_shape=(...]
    reduce_sum x3 -> x0, other arithmetic: 5.93 us -> none  [attend_block(): totals = totals * factor + jnp.sum(probs, axis=-1)]
    unnamed x22 -> x2, local copies, waits for them, and re-layouts: 7.85 us -> 3.53 us
where the time goes in v2:
time: 206 us
  Pallas kernels  197 us (96%)
  local copies, waits for them, and re-layouts  7.73 us (4%)
    pallas_call x1, Pallas kernels, local(): pl.pallas_call(functools.partial(core_kernel, n, heads_here), out_shape=(...  126 us
    pallas_call x1, Pallas kernels, local(): pl.pallas_call(functools.partial(enter_kernel, n, ndp, q_scale), out_shap...  71.2 us

profile of v2, /device:TPU:0, one launch (start us, length us, event | category | flops | bytes accessed | tf_op | source)
XLA Modules:
  0.0 205.8 jit_solution(12291026119953654844)
XLA Ops:
  0.6 1.3 reshape.16.gain
  1.9 1.3 reshape.19.gain
  3.2 1.6 copy.13.seg_rows
  4.8 71.2 %enter.1 = (bf16[768,512]{1,0:T(8,128)(2,1)}, bf16[8,512,256]{2,1,0:T(8,128)(2,1)}) custom-call(bf16[96,2048]{1,0:T(8,128)(2,1)} %hidden.3, bf16[1,2048]{1,0:T(2,128)(2,1)} %reshape.16.gain, bf16[1,512,256]{2,1,0:T(8,128)(2,1)} %prefix.1, bf16[2048,256]{1,0:T(8,128)(2,1)} %w_query.1, bf16[2048,256]{1,0:T(8,128)(2,1)} %w_keyval.1, s32[4]{0:T(128)} %owners.1), custom_call_target="tpu_custom_call" | custom-call | tf_op jit(solution)/shard_map/enter/pallas_call | solution.py:530
  76.0 126.3 %core.1 = (bf16[96,2048]{1,0:T(8,128)(2,1)}, bf16[96,2048]{1,0:T(8,128)(2,1)}) custom-call(bf16[768,512]{1,0:T(8,128)(2,1)} %get-tuple-element.6.projected, bf16[4096,256]{1,0:T(8,128)(2,1)} %bitcast.2, s32[768,1]{1,0:T(8,128)} %copy.13.seg_rows, s32[1,768]{1,0:T(1,128)} %seg_cols.1, bf16[256,2048]{1,0:T(8,128)(2,1)} %w_out.1, bf16[96,2048]{1,0:T(8,128)(2,1)} %hidden.3, ...), custom_call_target="tpu_custom_call" | custom-call | tf_op jit(solution)/shard_map/core/pallas_call | solution.py:543
  202.3 1.8 copy.16
  204.0 1.8 copy.17

commit v3 on v2

--- a/solution.py
+++ b/solution.py
@@ -255,13 +255,20 @@
         def _():
             self.forward(d, pc.a == pc.A - 1, self.down_in, self.down_out, self.copy_down)
 
-    def run(self, compute):
+    def run(self, compute, ready=0):
         pc = self.pc
         end = (pc.a == 0) | (pc.a == pc.A - 1)
 
         def step(k, carry):
             d = pc.far(k)
-            compute(d)
+            if ready:
+
+                @pl.when(k >= ready)
+                def _():
+                    compute(d)
+
+            else:
+                compute(d)
             self.start(d)
 
             @pl.when((k >= 1) & end)
@@ -329,29 +336,38 @@
             dma((A, side)), dma((A, side)), dma((A,)), dma((A,)), dma((A,)), dma((A,))]
 
 
-def enter_kernel(n, ndp, q_scale, hidden, gain, prefix, w_query, w_keyval, owners, projected, cached,
-                 normed, from_dp, dp_send, dp_recv, *sems):
+def layer_kernel(n, ndp, heads, q_scale, hidden, gain1, gain2, prefix, owners, w_query, w_keyval, seg, w_out,
+                 w_fc_hbm, w_proj_hbm, attended, layer_out, *scratch):
     pc = Place(n)
     dp = lax.axis_index("dp")
+    w_fc, w_proj, fc_sem, proj_sem, term, normed, normed2, middle, act, projected, cached = scratch[:11]
+    from_dp, dp_send, dp_recv = scratch[11:14]
     greet(pc, ndp)
     rows, width = hidden.shape
     slab = pc.B * rows
+    row_len = projected.shape[0]
     query_cols = w_query.shape[1]
+    head = query_cols // heads
+    span = pc.B * cached.shape[1]
 
     def to_dp(o):
         return remote(prefix.at[0], from_dp.at[dp], dp_send.at[o - 1], dp_recv.at[dp],
                       {"dp": (dp + o) % ndp})
 
-    gains = gain[...].astype(jnp.float32)
+    gains = gain1[...].astype(jnp.float32).reshape(1, width)
 
     def first(part):
         normed[pc.me, part, :] = norm_rows(hidden[part, :].astype(jnp.float32), gains)
 
     row_loop(rows, first)
-    tokens = Gather(pc, normed, *sems[:4])
+    tokens = Gather(pc, normed, *scratch[14:18])
     tokens.start()
     for o in range(1, ndp):
         to_dp(o).start()
+    load_fc = pltpu.make_async_copy(w_fc_hbm, w_fc, fc_sem)
+    load_proj = pltpu.make_async_copy(w_proj_hbm, w_proj, proj_sem)
+    load_fc.start()
+    load_proj.start()
     from_dp[dp] = prefix[0]
 
     def project(d):
@@ -374,40 +390,15 @@
         remote(prefix.at[0], from_dp.at[src], dp_send.at[0], dp_recv.at[src],
                {"dp": (dp + 1) % ndp}).wait_recv()
     cached[pc.me] = from_dp[owners[dp]]
-    keys = Gather(pc, cached, *sems[4:])
+    keys = Gather(pc, cached, *scratch[18:22])
     keys.start()
     project(pc.far(1))
     keys.round(1)
     project(pc.far(0))
-    for r in range(2, pc.A):
-        keys.round(r)
-    for a0 in range(pc.A):
-        keys.pair_arrived(a0)
-    tokens.finish()
-    keys.finish()
-    for o in range(1, ndp):
-        to_dp(o).wait_send()
-
-
-def core_kernel(n, heads, projected, cached, seg_rows, seg_cols, w_out, hidden, gain, w_fc_hbm, w_proj_hbm,
-                attended, layer_out, *scratch):
-    pc = Place(n)
-    w_fc, w_proj, fc_sem, proj_sem, term, term2, normed, middle, act = scratch[:9]
-    greet(pc)
-    load_fc = pltpu.make_async_copy(w_fc_hbm, w_fc, fc_sem)
-    load_proj = pltpu.make_async_copy(w_proj_hbm, w_proj, proj_sem)
-    load_fc.start()
-    load_proj.start()
-    rows, width = hidden.shape
-    slab = pc.B * rows
-    row_len = projected.shape[0]
-    head = cached.shape[1] // 2
-    q_cols = heads * head
-    span = min(1024, cached.shape[0])
-
-    def block(q, state, keys, values, allowed):
+
+    def block(q, state, keys_here, values, allowed):
         top, total, weighted = state
-        scores = lax.dot_general(q, keys, (((1,), (1,)), ((), ())), preferred_element_type=jnp.float32)
+        scores = lax.dot_general(q, keys_here, (((1,), (1,)), ((), ())), preferred_element_type=jnp.float32)
         if allowed is not None:
             scores = jnp.where(allowed[None], scores.reshape(heads, slab, -1), -jnp.inf)
             scores = scores.reshape(heads * slab, -1)
@@ -420,55 +411,77 @@
         )
         return new_top, total, weighted
 
-    def emit(left, weights, cols, target, d):
+    def emit(left, weights, d):
         wide = min(512, width)
 
         def column(c, carry):
             here = pl.ds(pl.multiple_of(c * wide, wide), wide)
             out = jnp.dot(left, weights[:, here], preferred_element_type=jnp.float32)
-            target[pl.ds(d * pc.B, pc.B), :, here] = out.astype(jnp.bfloat16).reshape(pc.B, rows, wide)
+            term[pl.ds(d * pc.B, pc.B), :, here] = out.astype(jnp.bfloat16).reshape(pc.B, rows, wide)
             return carry
 
         lax.fori_loop(0, width // wide, column, 0)
 
-    def attend(d):
+    def stacked(d):
         here = pl.ds(pl.multiple_of(d * slab, slab), slab)
-        q = jnp.concatenate([projected[here, h * head : (h + 1) * head] for h in range(heads)], axis=0)
+        return jnp.concatenate([projected[here, h * head : (h + 1) * head] for h in range(heads)], axis=0)
+
+    def over_suffix(d, q):
         state = (
             jnp.full((heads * slab, 1), -jnp.inf, jnp.float32),
             jnp.zeros((heads * slab, 1), jnp.float32),
             jnp.zeros((heads * slab, head), jnp.float32),
         )
-
-        def over(i, state):
-            part = pl.ds(pl.multiple_of(i * span, span), span)
-            return block(q, state, cached[part, :head], cached[part, head:], None)
-
-        state = lax.fori_loop(0, cached.shape[0] // span, over, state)
-        place = d * slab + lax.broadcasted_iota(jnp.int32, (slab, row_len), 0)
+        spot = d * slab + lax.broadcasted_iota(jnp.int32, (slab, row_len), 0)
         other = lax.broadcasted_iota(jnp.int32, (slab, row_len), 1)
-        allowed = (other <= place) & (seg_rows[here, :] == seg_cols[...])
-        top, total, weighted = block(
-            q, state, projected[:, q_cols : q_cols + head], projected[:, q_cols + head :], allowed
-        )
+        ids = seg[...].astype(jnp.float32)
+        mine = jnp.sum(jnp.where(other == spot, ids, 0.0), axis=1, keepdims=True)
+        allowed = (other <= spot) & (mine == ids)
+        return block(q, state, projected[:, query_cols : query_cols + head],
+                     projected[:, query_cols + head :], allowed)
+
+    def over_prefix(e, q, state):
+        pair = cached[pl.ds(e * pc.B, pc.B)].reshape(span, 2 * head)
+        return block(q, state, pair[:, :head], pair[:, head:], None)
+
+    def heads_done(d, state):
+        _, total, weighted = state
         out = (weighted / total).astype(jnp.bfloat16)
         left = jnp.concatenate([out[h * slab : (h + 1) * slab] for h in range(heads)], axis=1)
-        emit(left, w_out, q_cols, term, d)
-
-    scatter = Scatter(pc, term, *scratch[9:20])
-    scatter.run(attend)
-    gains = gain[...].astype(jnp.float32)
+        emit(left, w_out, d)
+
+    lead = pc.far(0)
+    q_lead = stacked(lead)
+    state = over_suffix(lead, q_lead)
+    for r in range(1, pc.A + 1):
+        e = pc.far(pc.A - r)
+        keys.pair_arrived(e)
+        state = over_prefix(e, q_lead, state)
+        if r + 1 < pc.A:
+            keys.round(r + 1)
+    heads_done(lead, state)
+
+    def attend(d):
+        q = stacked(d)
+        state = over_suffix(d, q)
+        state = lax.fori_loop(0, pc.A, lambda e, state: over_prefix(e, q, state), state)
+        heads_done(d, state)
+
+    scatter = Scatter(pc, term, *scratch[26:37])
+    scatter.run(attend, ready=1)
+    gains2 = gain2[...].astype(jnp.float32).reshape(1, width)
 
     def use(part, total):
         out = total.astype(jnp.bfloat16)
         attended[part, :] = out
         mid = (hidden[part, :].astype(jnp.float32) + out.astype(jnp.float32)).astype(jnp.bfloat16)
         middle[part, :] = mid
-        normed[pc.me, part, :] = norm_rows(mid.astype(jnp.float32), gains)
+        normed2[pc.me, part, :] = norm_rows(mid.astype(jnp.float32), gains2)
 
     scatter.result(use)
-    gather = Gather(pc, normed, *scratch[20:24])
+    gather = Gather(pc, normed2, *scratch[22:26])
     gather.start()
+    scatter.finish()
     load_fc.wait()
     load_proj.wait()
     units = w_fc.shape[1]
@@ -480,7 +493,7 @@
 
         def column(c, carry):
             cols = pl.ds(pl.multiple_of(c * wide, wide), wide)
-            left = normed[pl.ds(d * pc.B, pc.B)].reshape(slab, width)
+            left = normed2[pl.ds(d * pc.B, pc.B)].reshape(slab, width)
             out = jnp.dot(left, w_fc[:, cols], preferred_element_type=jnp.float32)
             act[here, cols] = jax.nn.gelu(out, approximate=True).astype(jnp.bfloat16)
             return carry
@@ -494,18 +507,26 @@
 
     def contract(d):
         here = pl.ds(pl.multiple_of(d * slab, slab), slab)
-        emit(act[here, :], w_proj, units, term2, d)
-
-    scatter2 = Scatter(pc, term2, *scratch[24:])
+        emit(act[here, :], w_proj, d)
+
+    scatter2 = Scatter(pc, term, *scratch[37:])
     scatter2.run(contract)
 
     def last(part, total):
         layer_out[part, :] = (middle[part, :].astype(jnp.float32) + total).astype(jnp.bfloat16)
 
     scatter2.result(last)
-    scatter.finish()
+    tokens.finish()
+    keys.finish()
+    for o in range(1, ndp):
+        to_dp(o).wait_send()
     gather.finish()
     scatter2.finish()
+
+
+def hand_on(attended, layer_out, attended_to, layer_to):
+    attended_to[...] = attended[...]
+    layer_to[...] = layer_out[...]
 
 
 VM = pl.BlockSpec(memory_space=pltpu.VMEM)
@@ -527,32 +548,27 @@
     bf = jnp.bfloat16
     dma = pltpu.SemaphoreType.DMA
     any_space = pl.BlockSpec(memory_space=pl.ANY)
-    projected, cached = pl.pallas_call(
-        functools.partial(enter_kernel, n, ndp, q_scale),
-        out_shape=(jax.ShapeDtypeStruct((row_len, query_cols + 2 * head_size), bf),
-                   jax.ShapeDtypeStruct((n, span, 2 * head_size), bf)),
-        in_specs=[VM] * 5 + [pl.BlockSpec(memory_space=pltpu.SMEM)],
-        out_specs=(VM, VM),
-        scratch_shapes=[pltpu.VMEM((n, rows, width), bf), pltpu.VMEM((ndp, span, 2 * head_size), bf),
-                        dma((ndp,)), dma((ndp,))] + gather_sems(n) + gather_sems(n),
-        compiler_params=params(1),
-        name="enter",
-    )(hidden_in, norm1_gain.reshape(1, -1), prefix_kv, w_query, w_keyval, owner_ids)
     own = jax.ShapeDtypeStruct((rows, width), bf)
-    terms = pltpu.VMEM((n, rows, width), bf)
+    shards = pltpu.VMEM((n, rows, width), bf)
     attended, layer_out = pl.pallas_call(
-        functools.partial(core_kernel, n, heads_here),
+        functools.partial(layer_kernel, n, ndp, heads_here, q_scale),
         out_shape=(own, own),
-        in_specs=[VM] * 7 + [any_space] * 2,
+        in_specs=[VM] * 4 + [pl.BlockSpec(memory_space=pltpu.SMEM)] + [VM] * 4 + [any_space] * 2,
         out_specs=(VM, VM),
         scratch_shapes=[pltpu.VMEM(w_fc.shape, bf), pltpu.VMEM(w_proj.shape, bf), dma(()), dma(()),
-                        terms, terms, terms, pltpu.VMEM((rows, width), bf),
-                        pltpu.VMEM((row_len, w_fc.shape[1]), bf)]
-        + scatter_scratch(n, rows, width) + gather_sems(n) + scatter_scratch(n, rows, width),
-        compiler_params=params(2),
-        name="core",
-    )(projected, cached.reshape(n * span, 2 * head_size), segment_ids.reshape(-1, 1),
-      segment_ids.reshape(1, -1), w_out, hidden_in, norm2_gain.reshape(1, -1), w_fc, w_proj)
+                        shards, shards, shards, pltpu.VMEM((rows, width), bf),
+                        pltpu.VMEM((row_len, w_fc.shape[1]), bf),
+                        pltpu.VMEM((row_len, query_cols + 2 * head_size), bf),
+                        pltpu.VMEM((n, span, 2 * head_size), bf),
+                        pltpu.VMEM((ndp, span, 2 * head_size), bf), dma((ndp,)), dma((ndp,))]
+        + gather_sems(n) * 3 + scatter_scratch(n, rows, width) * 2,
+        compiler_params=params(1),
+        name="layer",
+    )(hidden_in, norm1_gain, norm2_gain, prefix_kv, owner_ids, w_query, w_keyval, segment_ids, w_out,
+      w_fc, w_proj)
+    attended, layer_out = pl.pallas_call(
+        hand_on, out_shape=(own, own), in_specs=[VM] * 2, out_specs=(VM, VM), name="hand_on",
+    )(attended, layer_out)
     return (layer_out, attended)
 
 

time: 206 us -> 190 us (0.922)
  local copies, waits for them, and re-layouts: 7.73 us -> 0 us
  Pallas kernels: 197 us -> 190 us
    pallas_call x2, Pallas kernels: 197 us -> 190 us  [the longest x1 188 us: local(): pl.pallas_call(functools.partial(layer_kernel, n, ndp, heads_here, q_scal...]
    reshape x3 -> x0, local copies, waits for them, and re-layouts: 4.19 us -> none  [the longest x1 1.62 us: local(): segment_ids.reshape(-1, 1)]
    unnamed x2 -> x0, local copies, waits for them, and re-layouts: 3.53 us -> none
where the time goes in v3:
time: 190 us
  Pallas kernels  190 us (100%)
    pallas_call x1, Pallas kernels, local(): pl.pallas_call(functools.partial(layer_kernel, n, ndp, heads_here, q_scal...  188 us

profile of v3, /device:TPU:0, one launch (start us, length us, event | category | flops | bytes accessed | tf_op | source)
XLA Modules:
  0.0 190.3 jit_solution(14212820748949305176)
XLA Ops:
  0.6 187.6 %layer.1 = (bf16[96,2048]{1,0:T(8,128)(2,1)}, bf16[96,2048]{1,0:T(8,128)(2,1)}) custom-call(bf16[96,2048]{1,0:T(8,128)(2,1)} %hidden.1, bf16[2048]{0:T(1024)(128)(2,1)} %gain1.1, bf16[2048]{0:T(1024)(128)(2,1)} %gain2.1, bf16[1,512,256]{2,1,0:T(8,128)(2,1)} %prefix.1, s32[4]{0:T(128)} %owners.1, bf16[2048,256]{1,0:T(8,128)(2,1)} %w_query.1, ...), custom_call_target="tpu_custom_call" | custom-call | tf_op jit(solution)/shard_map/layer/pallas_call | solution.py:553
  188.3 2.0 %hand_on.1 = (bf16[96,2048]{1,0:T(8,128)(2,1)}, bf16[96,2048]{1,0:T(8,128)(2,1)}) custom-call(bf16[96,2048]{1,0:T(8,128)(2,1)} %get-tuple-element.6.attended, bf16[96,2048]{1,0:T(8,128)(2,1)} %get-tuple-element.7.layer_out), custom_call_target="tpu_custom_call" | custom-call | tf_op jit(solution)/shard_map/hand_on/pallas_call | solution.py:569
